TPU v7x, 512 devices: a whole 4x4x16 slice. The times are simulated.
512 devices in a mesh: gx: 16 (over z), gy: 32 (over y, x, core).
Axes of the slice: x: 4, y: 4, z: 16, core: 2. Of those that a mesh axis runs over, the one named last changes fastest.
Arguments:
- noise: float32 [16, 512, 512], P('gx', 'gy'), may hold values from -6 to 6
- stencil: float32 [9], replicated, may hold values from 0.04 to 0.2
- mean_counts: float32 [4], replicated, may hold values from 0.5 to 4
- bias_one: float32 [4], replicated, may hold values from 1 to 2
- bias_two: float32 [4], replicated, may hold values from 0.05 to 0.3
- owner: int32 [32, 16, 4, 1], P('gy', 'gx'), may hold values from 0 to 15; in each aligned block of 4 rows (0 to 3, 4 to 7, ..., all dimensions but the last counted through in order) at most 2 rows name the same one
- depth: int32 [16, 32, 32], P('gx', None, 'gy'), may hold values from 0 to 3
- counts: int32 [16, 32, 32, 16, 128], P('gx', None, 'gy'), may hold values from 0 to 6
Outputs:
- gradient: float32 [16, 512, 512], P('gx', 'gy')
- density: float32 [16, 512, 512], P('gx', 'gy')
Inputs may be any that keep to these rules, and one draw needn't show every extreme that they name: Of the tiles of one device (aligned blocks of 4 rows), at most 2 name the same owner, and in every draw some owner is named exactly 2 times by one device.
All inputs are finite; a program needn't handle non-finite values.
Results may differ from a plain program's by a relative error of at most 0.0001.
Values sent between devices are 32-bit elements; how exact they have to be, the bound alone decides.
A program may use at most 64 MiB of HBM per device.

v0:
```python
import functools
import math

import jax
import jax.numpy as jnp
import ml_dtypes
import numpy as np
from jax import lax
from jax.experimental import pallas as pl
from jax.experimental.pallas import tpu as pltpu
from jax.sharding import PartitionSpec as P

MESH = pl.DeviceIdType.MESH
NG = 512
TC = 128
NT = 4
AMPLITUDE = 0.75
GROWTH = 7.0 / 8.0
UNIT = 2.0 * math.pi / NG
F32 = jnp.float32
BF16 = jnp.bfloat16


def halves(table):
    high = table.astype(ml_dtypes.bfloat16)
    low = (table - high.astype(np.float64)).astype(ml_dtypes.bfloat16)
    return high, low


def make_tables():
    y = np.arange(256)[:, None]
    lane = np.arange(256)[None, :]
    half = 8 * (lane // 16) + lane % 8
    part = (lane // 8) % 2
    w = []
    for odd in (0, 1):
        turn = (y * (2 * half + odd)) % NG
        w.append(np.where(part == 0, np.cos(UNIT * turn), -np.sin(UNIT * turn)))
    w_tab = np.stack([piece for table in w for piece in halves(table)])
    k = np.arange(64)[:, None]
    row = np.arange(64)[None, :]
    turn = (k * (2 * (row % 32) + row // 32)) % 64
    cs = np.concatenate([np.cos(2 * math.pi * turn / 64), np.sin(2 * math.pi * turn / 64)], 0)
    hi, lo = halves(cs)
    cs_tab = np.concatenate([hi, lo, hi], 1)
    hi, lo = halves(np.concatenate([cs[:64].T, cs[64:].T], 1))
    ct_tab = np.concatenate([hi, lo, hi], 1)
    d8 = np.zeros((8, 2, 8, 8, 2, 8))
    for xl in range(8):
        for q in range(8):
            co, si = np.cos(2 * math.pi * (q * xl % 8) / 8), np.sin(2 * math.pi * (q * xl % 8) / 8)
            for m in range(8):
                d8[xl, 0, m, q, 0, m] = co
                d8[xl, 1, m, q, 0, m] = si
                d8[xl, 1, m, q, 1, m] = co
                d8[xl, 0, m, q, 1, m] = -si
    d8 = d8.reshape(128, 128)
    minus_i = np.zeros((128, 128))
    for g in range(8):
        for m in range(8):
            minus_i[g * 16 + 8 + m, g * 16 + m] = 1.0
            minus_i[g * 16 + m, g * 16 + 8 + m] = -1.0
    d8_tab = np.stack(halves(np.concatenate([d8, minus_i @ d8], 0)))
    kk = np.arange(64)[:, None]
    xl = (np.arange(128) // 16)[None, :]
    tw_tab = np.stack([np.cos(UNIT * kk * xl), np.sin(UNIT * kk * xl)]).astype(np.float32)
    return w_tab, cs_tab, ct_tab, d8_tab, tw_tab


def split(x):
    high = x.astype(BF16)
    return high, (x - high.astype(F32)).astype(BF16)


def nn(a, b):
    return lax.dot_general(a, b, (((1,), (0,)), ((), ())), preferred_element_type=F32)


def nt(a, b):
    return lax.dot_general(a, b, (((1,), (1,)), ((), ())), preferred_element_type=F32)


def dot3(mul, x, high, low):
    x_high, x_low = split(x)
    return mul(x_high, high) + (mul(x_high, low) + mul(x_low, high))


def left3(table, x):
    x_high, x_low = split(x)
    return nn(table, jnp.concatenate([x_high, x_high, x_low], 0))


def rows_forward(v, w):
    low, high = v[:, :256], v[:, 256:]
    return jnp.concatenate([dot3(nn, low + high, w[0], w[1]), dot3(nn, low - high, w[2], w[3])], 1)


def rows_inverse(s, w):
    even, odd = dot3(nt, s[:, :256], w[0], w[1]), dot3(nt, s[:, 256:], w[2], w[3])
    return jnp.concatenate([even + odd, even - odd], 1)


def columns_forward(fields, cs, d8, tw):
    turned = left3(cs, jnp.concatenate(fields, 1))
    tc, ts = tw
    parts = []
    for f in range(len(fields)):
        a, b = turned[:64, 128 * f : 128 * f + 128], turned[64:, 128 * f : 128 * f + 128]
        parts.append(jnp.concatenate([tc * a - ts * b, tc * b + ts * a], 1))
    out = dot3(nn, jnp.concatenate(parts, 0), d8[0], d8[1])
    return [out[64 * f : 64 * f + 64] for f in range(len(fields))]


def columns_inverse(fields, ct, d8, tw):
    out = dot3(nt, jnp.concatenate(fields, 0), d8[0], d8[1])
    tc, ts = tw
    parts = []
    for f in range(len(fields)):
        a, b = out[64 * f : 64 * f + 64, :128], out[64 * f : 64 * f + 64, 128:]
        parts.append(jnp.concatenate([tc * a + ts * b, tc * b - ts * a], 0))
    back = left3(ct, jnp.concatenate(parts, 1))
    return [back[:, 128 * f : 128 * f + 128] for f in range(len(fields))]


def swap_parts(v, roll):
    lane = lax.broadcasted_iota(jnp.int32, v.shape, 1)
    return jnp.where(lane // 8 % 2 == 0, roll(v, v.shape[1] - 8, 1), roll(v, 8, 1))


def part_sign(shape):
    lane = lax.broadcasted_iota(jnp.int32, shape, 1)
    return jnp.where(lane // 8 % 2 == 0, -1.0, 1.0).astype(F32)


def times_ky(v, roll):
    lane = lax.broadcasted_iota(jnp.int32, (1, NG), 1)
    e = lane // 16
    ky = UNIT * (2 * (8 * (e % 16) + lane % 8) + e // 16).astype(F32)
    return part_sign((1, NG)) * ky * swap_parts(v, roll)


def filters(e):
    shape = (64, 128)
    k = lax.broadcasted_iota(jnp.int32, shape, 0)
    lane = lax.broadcasted_iota(jnp.int32, shape, 1)
    mx = k + 64 * (lane // 16)
    my = 2 * (8 * (e % 16) + lane % 8) + e // 16
    kx = UNIT * jnp.where(mx > NG // 2, mx - NG, mx).astype(F32)
    ky = UNIT * my.astype(F32)
    k2 = kx * kx + ky * ky
    safe = jnp.where(k2 > 0, k2, 1.0)
    inverse_sq = jnp.where(k2 > 0, 1.0 / safe, 0.0)
    envelope = jnp.where(mx != NG // 2, AMPLITUDE * jnp.sqrt(k2) / (1.0 + k2), 0.0)
    weight = jnp.where(my == 0, 1.0, 2.0).astype(F32) / (NG * NG)
    base = weight * envelope
    return base, base * kx * inverse_sq, base * kx, base * inverse_sq


def turn_vreg(x, roll):
    row = lax.broadcasted_iota(jnp.int32, (8, 128), 0)
    group = lax.broadcasted_iota(jnp.int32, (8, 128), 1) // 16
    for s in (1, 2, 4):
        row_bit, group_bit = row // s % 2, group // s % 2
        down = roll(roll(x, 8 - s, 0), 16 * s, 1)
        up = down if s == 4 else roll(roll(x, s, 0), 128 - 16 * s, 1)
        x = jnp.where(row_bit == group_bit, x, jnp.where(row_bit == 0, down, up))
    return x


def turn_list(vs, roll):
    group = lax.broadcasted_iota(jnp.int32, vs[0].shape, 1) // 16
    vs = list(vs)
    for s in (1, 2, 4):
        low = group // s % 2 == 0
        for i in range(8):
            if i & s == 0:
                a, b = vs[i], vs[i + s]
                vs[i] = jnp.where(low, a, roll(b, 16 * s, 1))
                vs[i + s] = jnp.where(low, roll(a, 128 - 16 * s, 1), b)
    return vs


def panels(nat, start, stop):
    return jnp.concatenate([nat[72 * eb + start : 72 * eb + stop, :] for eb in range(4)], 1)


def halo_out(backs, roll):
    group = lax.broadcasted_iota(jnp.int32, (32, 128), 1) // 16
    before = after = jnp.zeros((32, 128), F32)
    for f, back in enumerate(backs):
        before = jnp.where(group == 2 * f, roll(back[32:], 16 * ((2 * f - 7) % 8), 1), before)
        shifted = roll(back[:32], 16 * (2 * f + 1), 1)
        after = jnp.where(group == 2 * f + 1, shifted, after)
    return jnp.where(group % 2 == 0, roll(before, 1, 0), roll(after, 31, 0))


def halo_in(mains, halo, roll):
    group = lax.broadcasted_iota(jnp.int32, (32, 128), 1) // 16
    from_next, from_prev = roll(halo, 31, 0), roll(halo, 1, 0)
    out = []
    for f, main in enumerate(mains):
        top = main[:32] + jnp.where(group == 0, roll(from_prev, 16 * ((8 - 2 * f - 1) % 8), 1), 0.0)
        end = main[32:] + jnp.where(group == 7, roll(from_next, 16 * (7 - 2 * f), 1), 0.0)
        out.append(jnp.concatenate([top, end], 0))
    return out


def spread(nat, halo, w, roll):
    rows = [nat[0:48], times_ky(nat[48:64], roll), times_ky(nat[0:16], roll), halo, times_ky(halo, roll)]
    return rows_inverse(jnp.concatenate(rows, 0), w)


def field_rows(out):
    main = (out[0:16], out[16:32], out[32:48], out[48:64], out[64:80])
    edge = (out[80:82], out[82:84], out[84:86], out[94:96], out[88:90])
    return main, edge


def density_of(fields):
    linear, shift_x, slope_x, shift_y, slope_y = fields
    return linear + GROWTH * linear * linear - (shift_x * slope_x + shift_y * slope_y)


def adjoints_of(pulled, fields):
    linear, shift_x, slope_x, shift_y, slope_y = fields
    return (
        pulled * (1.0 + 2.0 * GROWTH * linear),
        -pulled * slope_x,
        -pulled * shift_x,
        -pulled * slope_y,
        -pulled * shift_y,
    )


def adjoint_rows(main, edge, w, roll):
    none = jnp.zeros((2, NG), F32)
    rows = list(main) + [edge[0], edge[1], edge[2], none, edge[4], none, none, edge[3]]
    out = rows_forward(jnp.concatenate(rows, 0), w)
    nat = jnp.concatenate(
        [out[0:16] - times_ky(out[64:80], roll), out[16:48], -times_ky(out[48:64], roll)], 0
    )
    return nat, out[80:88] - times_ky(out[88:96], roll)


def kernel(
    n_gx, n_gy, noise_ref, stencil_ref, mean_ref, one_ref, two_ref, owner_ref, depth_ref, counts_ref,
    w_ref, cs_ref, ct_ref, d8_ref, tw_ref, grad_ref, dens_ref,
    s1, r1, s2, r2, s3, r3, s4, r4, nat, field, frame, dsend, dgot, cgot,
    send_sem, recv_sem, zsend_sem, zrecv_sem,
):
    roll = pltpu.roll
    gx, gy = lax.axis_index("gx"), lax.axis_index("gy")

    barrier = pltpu.get_barrier_semaphore()

    @pl.loop(1, n_gy)
    def _(off):
        pl.semaphore_signal(barrier, inc=1, device_id=(gx, lax.rem(gy + off, n_gy)), device_id_type=MESH)

    @pl.loop(1, n_gx)
    def _(off):
        pl.semaphore_signal(barrier, inc=1, device_id=(lax.rem(gx + off, n_gx), gy), device_id_type=MESH)

    def exchange(phase, src, dst, pitch, count):
        @pl.loop(1, n_gy)
        def _(off):
            to = lax.rem(gy + off, n_gy)
            pltpu.make_async_remote_copy(
                src_ref=src.at[pl.ds(pl.multiple_of(to * pitch, 8), count)],
                dst_ref=dst.at[pl.ds(pl.multiple_of(gy * pitch, 8), count)],
                send_sem=send_sem.at[phase],
                recv_sem=recv_sem.at[phase],
                device_id=(gx, to),
                device_id_type=MESH,
            ).start()

        mine = pl.ds(pl.multiple_of(gy * pitch, 8), pitch)
        dst[mine, :] = src[mine, :]

    def everything(phase, buf, count):
        rows = pl.ds(0, (n_gy - 1) * count)
        return pltpu.make_async_remote_copy(
            src_ref=buf.at[rows],
            dst_ref=buf.at[rows],
            send_sem=send_sem.at[phase],
            recv_sem=recv_sem.at[phase],
            device_id=(gx, lax.rem(gy + 1, n_gy)),
            device_id_type=MESH,
        )

    w = [w_ref.at[i] for i in range(4)]
    w = [ref[...] for ref in w]

    spec = rows_forward(noise_ref[...], w)
    for xh in range(2):
        for eb in range(4):
            block = spec[8 * xh : 8 * xh + 8, 128 * eb : 128 * eb + 128]
            s1[pl.ds(64 * eb + xh, 8, stride=8), :] = turn_vreg(block, roll)
    wide = jnp.broadcast_to(depth_ref[...], (2 * n_gx, 128))
    for slot in range(2 * n_gx):
        dsend[slot // 2, slot % 2 : slot % 2 + 1, :] = wide[slot : slot + 1, :]

    pl.semaphore_wait(barrier, n_gy - 1 + n_gx - 1)
    exchange(0, s1, r1, 8, 2)

    @pl.loop(1, n_gx)
    def _(off):
        to = lax.rem(gx + off, n_gx)
        pltpu.make_async_remote_copy(
            src_ref=counts_ref.at[pl.ds(2 * to, 2)],
            dst_ref=cgot.at[pl.ds(2 * gx, 2)],
            send_sem=zsend_sem.at[0],
            recv_sem=zrecv_sem.at[0],
            device_id=(to, gy),
            device_id_type=MESH,
        ).start()
        pltpu.make_async_remote_copy(
            src_ref=dsend.at[to],
            dst_ref=dgot.at[gx],
            send_sem=zsend_sem.at[1],
            recv_sem=zrecv_sem.at[1],
            device_id=(to, gy),
            device_id_type=MESH,
        ).start()

    own = pltpu.make_async_copy(counts_ref.at[pl.ds(2 * gx, 2)], cgot.at[pl.ds(2 * gx, 2)], zsend_sem.at[2])
    own.start()
    dgot[gx] = dsend[gx]

    flt = filters(gy)
    tw = (tw_ref[0], tw_ref[1])
    d8 = (d8_ref[0], d8_ref[1])
    cs, ct = cs_ref[...], ct_ref[...]
    sign = part_sign((64, 128))

    everything(0, r1, 2).wait_recv()
    packed = jnp.concatenate([r1[pl.ds(xh, 32, stride=8), :] for xh in range(2)], 0)
    modes = columns_forward([packed], cs, d8, tw)[0]
    turned = sign * swap_parts(modes, roll)
    backs = columns_inverse([flt[0] * modes, flt[1] * turned, flt[2] * turned, flt[3] * modes], ct, d8, tw)
    for f in range(4):
        for xh in range(2):
            s2[pl.ds(2 * f + xh, 32, stride=16), :] = backs[f][32 * xh : 32 * xh + 32]
    s2[pl.ds(8, 32, stride=16), :] = halo_out(backs, roll)
    exchange(1, s2, r2, 16, 9)

    everything(1, r2, 9).wait_recv()
    for eb in range(4):
        outs = turn_list([r2[128 * eb + 16 * i : 128 * eb + 16 * i + 8, :] for i in range(8)], roll)
        for xl in range(8):
            nat[pl.ds(72 * eb + xl, 8, stride=8), :] = outs[xl]
        nat[72 * eb + 64 : 72 * eb + 72, :] = turn_vreg(r2[pl.ds(128 * eb + 8, 8, stride=16), :], roll)
    field[...] = spread(panels(nat, 0, 64), panels(nat, 64, 72), w, roll)
    main, edge = field_rows(field)
    dens = density_of(main)
    dens_edge = density_of(edge)
    dens_ref[...] = dens
    frame[8:24, :] = dens
    frame[7:8, :] = dens_edge[0:1]
    frame[24:25, :] = dens_edge[1:2]
    cols = []
    for b in range(3):
        cols.append(sum(stencil_ref[3 * a + b] * frame[7 + a : 23 + a, :] for a in range(3)))
    smooth = roll(cols[0], 1, 1) + cols[1] + roll(cols[2], NG - 1, 1)

    got = pltpu.make_async_remote_copy(
        src_ref=cgot.at[pl.ds(0, 2 * n_gx - 2)],
        dst_ref=cgot.at[pl.ds(0, 2 * n_gx - 2)],
        send_sem=zsend_sem.at[0],
        recv_sem=zrecv_sem.at[0],
        device_id=(lax.rem(gx + 1, n_gx), gy),
        device_id_type=MESH,
    )
    got_depth = pltpu.make_async_remote_copy(
        src_ref=dgot.at[pl.ds(0, n_gx - 1)],
        dst_ref=dgot.at[pl.ds(0, n_gx - 1)],
        send_sem=zsend_sem.at[1],
        recv_sem=zrecv_sem.at[1],
        device_id=(lax.rem(gx + 1, n_gx), gy),
        device_id_type=MESH,
    )
    own.wait()
    got.wait_recv()
    got_depth.wait_recv()
    frame[0:8, :] = jnp.zeros((8, NG), F32)
    frame[24:32, :] = jnp.zeros((8, NG), F32)
    for t in range(NT):
        holder = owner_ref[t]
        rank = jnp.int32(0)
        for t2 in range(t):
            rank = rank + jnp.where(owner_ref[t2] == holder, 1, 0)
        seen = cgot[2 * holder + rank].astype(F32)
        classes = dgot[holder]
        e = jnp.where(rank == 0, classes[0:1, :], classes[1:2, :])

        def pick(ref):
            out = jnp.full((1, 128), ref[0], F32)
            for value in range(1, 4):
                out = jnp.where(e == value, ref[value], out)
            return out

        level, lin, quad = pick(mean_ref), pick(one_ref), pick(two_ref)
        cell = smooth[:, TC * t : TC * t + TC]
        rate = level * jnp.exp(lin * cell + quad * cell * cell)
        frame[8:24, TC * t : TC * t + TC] = (seen - rate) * (lin + 2.0 * quad * cell)

    cols = []
    for b in range(3):
        inner = sum(stencil_ref[3 * a + b] * frame[9 - a : 25 - a, :] for a in range(3))
        outer = jnp.concatenate([stencil_ref[b] * frame[8:9, :], stencil_ref[6 + b] * frame[23:24, :]], 0)
        cols.append((inner, outer))
    pulled = roll(cols[0][0], NG - 1, 1) + cols[1][0] + roll(cols[2][0], 1, 1)
    pulled_edge = roll(cols[0][1], NG - 1, 1) + cols[1][1] + roll(cols[2][1], 1, 1)
    main, edge = field_rows(field)
    rows, halo = adjoint_rows(adjoints_of(pulled, main), adjoints_of(pulled_edge, edge), w, roll)
    for eb in range(4):
        cols = slice(128 * eb, 128 * eb + 128)
        nat[72 * eb : 72 * eb + 64, :] = rows[:, cols]
        outs = turn_list([nat[pl.ds(72 * eb + xl, 8, stride=8), :] for xl in range(8)], roll)
        for i in range(8):
            s3[128 * eb + 16 * i : 128 * eb + 16 * i + 8, :] = outs[i]
        s3[pl.ds(128 * eb + 8, 8, stride=16), :] = turn_vreg(halo[:, cols], roll)
    exchange(2, s3, r3, 16, 9)

    everything(2, r3, 9).wait_recv()
    mains = [
        jnp.concatenate([r3[pl.ds(2 * f + xh, 32, stride=16), :] for xh in range(2)], 0) for f in range(4)
    ]
    mains = halo_in(mains, r3[pl.ds(8, 32, stride=16), :], roll)
    modes = columns_forward(mains, cs, d8, tw)
    summed = flt[0] * modes[0] + flt[3] * modes[3] - sign * swap_parts(flt[1] * modes[1] + flt[2] * modes[2], roll)
    back = columns_inverse([summed], ct, d8, tw)[0]
    for xh in range(2):
        s4[pl.ds(xh, 32, stride=8), :] = back[32 * xh : 32 * xh + 32]
    exchange(3, s4, r4, 8, 2)

    everything(3, r4, 2).wait_recv()
    for xh in range(2):
        for eb in range(4):
            block = r4[pl.ds(64 * eb + xh, 8, stride=8), :]
            nat[72 * eb + 8 * xh : 72 * eb + 8 * xh + 8, :] = turn_vreg(block, roll)
    grad_ref[...] = rows_inverse(panels(nat, 0, 16), w) - noise_ref[...]

    for phase, (buf, count) in enumerate(((s1, 2), (s2, 9), (s3, 9), (s4, 2))):
        everything(phase, buf, count).wait_send()
    got.wait_send()
    got_depth.wait_send()


def local(tables, n_gx, n_gy, noise, stencil, mean_counts, bias_one, bias_two, owner, depth, counts):
    rows = noise.shape[1]
    slots = counts.shape[1]
    vmem = pl.BlockSpec(memory_space=pltpu.VMEM)
    smem = pl.BlockSpec(memory_space=pltpu.SMEM)
    out = jax.ShapeDtypeStruct((rows, NG), F32)
    grad, dens = pl.pallas_call(
        functools.partial(kernel, n_gx, n_gy),
        out_shape=(out, out),
        in_specs=[vmem] + [smem] * 5 + [vmem, pl.BlockSpec(memory_space=pl.ANY)] + [vmem] * 5,
        out_specs=(vmem, vmem),
        scratch_shapes=[
            pltpu.VMEM((256, 128), F32),
            pltpu.VMEM((256, 128), F32),
            pltpu.VMEM((512, 128), F32),
            pltpu.VMEM((512, 128), F32),
            pltpu.VMEM((512, 128), F32),
            pltpu.VMEM((512, 128), F32),
            pltpu.VMEM((256, 128), F32),
            pltpu.VMEM((256, 128), F32),
            pltpu.VMEM((288, 128), F32),
            pltpu.VMEM((96, NG), F32),
            pltpu.VMEM((32, NG), F32),
            pltpu.VMEM((n_gx, 8, 128), jnp.int32),
            pltpu.VMEM((n_gx, 8, 128), jnp.int32),
            pltpu.VMEM((slots, rows, TC), jnp.int32),
            pltpu.SemaphoreType.DMA((4,)),
            pltpu.SemaphoreType.DMA((4,)),
            pltpu.SemaphoreType.DMA((3,)),
            pltpu.SemaphoreType.DMA((2,)),
        ],
        compiler_params=pltpu.CompilerParams(collective_id=0, has_side_effects=True),
        name="posterior",
    )(
        noise.reshape(rows, NG),
        stencil,
        mean_counts,
        bias_one,
        bias_two,
        owner.reshape(-1),
        depth.reshape(slots, 1),
        counts.reshape(slots, rows, TC),
        *[jnp.asarray(table) for table in tables],
    )
    return grad[None], dens[None]


def solution(mesh):
    return jax.shard_map(
        functools.partial(local, make_tables(), mesh.shape["gx"], mesh.shape["gy"]),
        mesh=mesh,
        in_specs=(
            P("gx", "gy", None),
            P(),
            P(),
            P(),
            P(),
            P("gy", "gx", None, None),
            P("gx", None, "gy"),
            P("gx", None, "gy", None, None),
        ),
        out_specs=(P("gx", "gy", None), P("gx", "gy", None)),
        check_vma=False,
    )
```

profile of v0, /device:TPU:1, one launch (start us, length us, event | category | flops | bytes accessed | tf_op | source)
XLA Modules:
  0.0 54.1 jit_solution(16753082244504326864)
XLA Ops:
  0.6 0.0 copy-start.1
  0.6 0.6 %copy-done.1 = s32[1,32,1]{1,2,0:T(1,128)S(1)} copy-done((s32[1,32,1]{1,2,0:T(1,128)S(1)}, s32[1,32,1]{1,2,0:T(1,128)}, u32[]{:S(2)}) %copy-start.1) | copy-done | bytes 152
  1.3 0.7 %copy.15.depth_ref = s32[32,1]{1,0:T(8,128)} copy(s32[32,1]{0,1:T(1,128)S(1)} %bitcast.11) | data formatting | bytes 256 | tf_op jit(solution)/shard_map/reshape | solution.py:490
  2.0 50.1 %posterior.1 = (f32[16,512]{1,0:T(8,128)}, f32[16,512]{1,0:T(8,128)}) custom-call(f32[16,512]{1,0:T(8,128)} %bitcast.7, f32[9]{0:T(128)} %stencil_ref.1, f32[4]{0:T(128)} %mean_ref.1, f32[4]{0:T(128)} %one_ref.1, f32[4]{0:T(128)} %two_ref.1, s32[4]{0:T(128)} %bitcast.10, s32[32,1]{1,0:T(8,128)} %copy.15.depth_ref, s32[32,16,128]{2,1,0:T(8,128)} %bitcast.6, ...), custom_call_target="tpu_custom_call" | custom-call | tf_op jit(solution)/shard_map/posterior/pallas_call | solution.py:456
  52.1 0.0 copy-start
  52.1 1.4 %copy.18 = f32[1,16,512]{2,1,0:T(8,128)} copy(f32[1,16,512]{2,1,0:T(8,128)} %bitcast.9) | data formatting | bytes 65536
  53.5 0.0 copy-done
  53.5 0.6 %copy.19 = f32[1,16,512]{2,1,0:T(8,128)} copy(f32[1,16,512]{2,1,0:T(8,128)S(1)} %bitcast.8) | data formatting | bytes 65536
Async XLA Ops:
  0.6 0.7 %copy-start.1 = (s32[1,32,1]{1,2,0:T(1,128)S(1)}, s32[1,32,1]{1,2,0:T(1,128)}, u32[]{:S(2)}) copy-start(s32[1,32,1]{1,2,0:T(1,128)} %param.19) | copy-start | bytes 388
  52.1 1.4 %copy-start = (f32[16,512]{1,0:T(8,128)S(1)}, f32[16,512]{1,0:T(8,128)}, u32[]{:S(2)}) copy-start(f32[16,512]{1,0:T(8,128)} %get-tuple-element.5) | copy-start | bytes 98308
where the time goes:
time: 54.4 us; the launch traced here: 54.1 us
  Pallas kernels  50.1 us (92%)
  local copies, waits for them, and re-layouts  3.34 us (6%)
  between operations  0.66 us (1%)
    pallas_call x1, Pallas kernels, local(): pl.pallas_call(functools.partial(kernel, n_gx, n_gy), out_shape=(out, out...  50.1 us
    unnamed x6, local copies, waits for them, and re-layouts  2.65 us

commit v1 on v0

--- a/solution.py
+++ b/solution.py
@@ -242,9 +242,22 @@
     return nat, out[80:88] - times_ky(out[88:96], roll)
 
 
+def far(i):
+    return 8 + jnp.where(i % 2 == 0, i // 2, -(i + 1) // 2)
+
+
+def plane_peers(gy):
+    y, x, core = gy // 8, gy // 2 % 4, gy % 2
+    steps = [(dy, dx, dc) for dy in range(4) for dx in range(4) for dc in range(2)][1:]
+    steps.sort(key=lambda step: -(min(step[0], 4 - step[0]) + min(step[1], 4 - step[1])))
+    return [(y + dy) % 4 * 8 + (x + dx) % 4 * 2 + (core + dc) % 2 for dy, dx, dc in steps]
+
+
 def kernel(
-    n_gx, n_gy, noise_ref, stencil_ref, mean_ref, one_ref, two_ref, owner_ref, depth_ref, counts_ref,
-    w_ref, cs_ref, ct_ref, d8_ref, tw_ref, grad_ref, dens_ref,
+    n_gx, n_gy, noise_hbm, stencil_hbm, mean_hbm, one_hbm, two_hbm, owner_hbm, depth_hbm, counts_ref,
+    w_hbm, cs_hbm, ct_hbm, d8_hbm, tw_hbm, grad_ref, dens_ref,
+    noise_ref, stencil_ref, mean_ref, one_ref, two_ref, owner_ref, depth_ref,
+    w_ref, cs_ref, ct_ref, d8_ref, tw_ref, in_sem,
     s1, r1, s2, r2, s3, r3, s4, r4, nat, field, frame, dsend, dgot, cgot,
     send_sem, recv_sem, zsend_sem, zrecv_sem,
 ):
@@ -253,18 +266,28 @@
 
     barrier = pltpu.get_barrier_semaphore()
 
-    @pl.loop(1, n_gy)
-    def _(off):
-        pl.semaphore_signal(barrier, inc=1, device_id=(gx, lax.rem(gy + off, n_gy)), device_id_type=MESH)
-
-    @pl.loop(1, n_gx)
-    def _(off):
-        pl.semaphore_signal(barrier, inc=1, device_id=(lax.rem(gx + off, n_gx), gy), device_id_type=MESH)
+    @pl.loop(0, n_gx - 1)
+    def _(i):
+        pl.semaphore_signal(barrier, inc=1, device_id=(lax.rem(gx + far(i), n_gx), gy), device_id_type=MESH)
+
+    for to in plane_peers(gy):
+        pl.semaphore_signal(barrier, inc=1, device_id=(gx, to), device_id_type=MESH)
+
+    loads = [
+        pltpu.make_async_copy(src, dst, in_sem.at[i])
+        for i, (src, dst) in enumerate(
+            (
+                (noise_hbm, noise_ref), (w_hbm, w_ref), (depth_hbm, depth_ref), (cs_hbm, cs_ref), (ct_hbm, ct_ref),
+                (d8_hbm, d8_ref), (tw_hbm, tw_ref), (stencil_hbm, stencil_ref), (mean_hbm, mean_ref),
+                (one_hbm, one_ref), (two_hbm, two_ref), (owner_hbm, owner_ref),
+            )
+        )
+    ]
+    for load in loads:
+        load.start()
 
     def exchange(phase, src, dst, pitch, count):
-        @pl.loop(1, n_gy)
-        def _(off):
-            to = lax.rem(gy + off, n_gy)
+        for to in plane_peers(gy):
             pltpu.make_async_remote_copy(
                 src_ref=src.at[pl.ds(pl.multiple_of(to * pitch, 8), count)],
                 dst_ref=dst.at[pl.ds(pl.multiple_of(gy * pitch, 8), count)],
@@ -288,24 +311,25 @@
             device_id_type=MESH,
         )
 
-    w = [w_ref.at[i] for i in range(4)]
-    w = [ref[...] for ref in w]
+    loads[0].wait()
+    loads[1].wait()
+    w = [w_ref[i] for i in range(4)]
 
     spec = rows_forward(noise_ref[...], w)
     for xh in range(2):
         for eb in range(4):
             block = spec[8 * xh : 8 * xh + 8, 128 * eb : 128 * eb + 128]
             s1[pl.ds(64 * eb + xh, 8, stride=8), :] = turn_vreg(block, roll)
-    wide = jnp.broadcast_to(depth_ref[...], (2 * n_gx, 128))
+    loads[2].wait()
     for slot in range(2 * n_gx):
-        dsend[slot // 2, slot % 2 : slot % 2 + 1, :] = wide[slot : slot + 1, :]
+        dsend[slot // 2, slot % 2 : slot % 2 + 1, :] = jnp.full((1, 128), depth_ref[slot], jnp.int32)
 
     pl.semaphore_wait(barrier, n_gy - 1 + n_gx - 1)
     exchange(0, s1, r1, 8, 2)
 
-    @pl.loop(1, n_gx)
-    def _(off):
-        to = lax.rem(gx + off, n_gx)
+    @pl.loop(0, n_gx - 1)
+    def _(i):
+        to = lax.rem(gx + far(i), n_gx)
         pltpu.make_async_remote_copy(
             src_ref=counts_ref.at[pl.ds(2 * to, 2)],
             dst_ref=cgot.at[pl.ds(2 * gx, 2)],
@@ -315,8 +339,8 @@
             device_id_type=MESH,
         ).start()
         pltpu.make_async_remote_copy(
-            src_ref=dsend.at[to],
-            dst_ref=dgot.at[gx],
+            src_ref=dsend.at[to, pl.ds(0, 2)],
+            dst_ref=dgot.at[gx, pl.ds(0, 2)],
             send_sem=zsend_sem.at[1],
             recv_sem=zrecv_sem.at[1],
             device_id=(to, gy),
@@ -325,9 +349,11 @@
 
     own = pltpu.make_async_copy(counts_ref.at[pl.ds(2 * gx, 2)], cgot.at[pl.ds(2 * gx, 2)], zsend_sem.at[2])
     own.start()
-    dgot[gx] = dsend[gx]
+    dgot[gx, 0:2, :] = dsend[gx, 0:2, :]
 
     flt = filters(gy)
+    for load in loads[3:]:
+        load.wait()
     tw = (tw_ref[0], tw_ref[1])
     d8 = (d8_ref[0], d8_ref[1])
     cs, ct = cs_ref[...], ct_ref[...]
@@ -372,8 +398,8 @@
         device_id_type=MESH,
     )
     got_depth = pltpu.make_async_remote_copy(
-        src_ref=dgot.at[pl.ds(0, n_gx - 1)],
-        dst_ref=dgot.at[pl.ds(0, n_gx - 1)],
+        src_ref=dgot.at[pl.ds(0, n_gx - 1), pl.ds(0, 2)],
+        dst_ref=dgot.at[pl.ds(0, n_gx - 1), pl.ds(0, 2)],
         send_sem=zsend_sem.at[1],
         recv_sem=zrecv_sem.at[1],
         device_id=(lax.rem(gx + 1, n_gx), gy),
@@ -451,14 +477,22 @@
     rows = noise.shape[1]
     slots = counts.shape[1]
     vmem = pl.BlockSpec(memory_space=pltpu.VMEM)
-    smem = pl.BlockSpec(memory_space=pltpu.SMEM)
     out = jax.ShapeDtypeStruct((rows, NG), F32)
     grad, dens = pl.pallas_call(
         functools.partial(kernel, n_gx, n_gy),
         out_shape=(out, out),
-        in_specs=[vmem] + [smem] * 5 + [vmem, pl.BlockSpec(memory_space=pl.ANY)] + [vmem] * 5,
+        in_specs=[pl.BlockSpec(memory_space=pltpu.HBM)] * 13,
         out_specs=(vmem, vmem),
         scratch_shapes=[
+            pltpu.VMEM((rows, NG), F32),
+            pltpu.SMEM((9,), F32),
+            pltpu.SMEM((4,), F32),
+            pltpu.SMEM((4,), F32),
+            pltpu.SMEM((4,), F32),
+            pltpu.SMEM((NT,), jnp.int32),
+            pltpu.SMEM((slots,), jnp.int32),
+            *[pltpu.VMEM(table.shape, table.dtype) for table in tables],
+            pltpu.SemaphoreType.DMA((12,)),
             pltpu.VMEM((256, 128), F32),
             pltpu.VMEM((256, 128), F32),
             pltpu.VMEM((512, 128), F32),
@@ -487,7 +521,7 @@
         bias_one,
         bias_two,
         owner.reshape(-1),
-        depth.reshape(slots, 1),
+        depth.reshape(slots),
         counts.reshape(slots, rows, TC),
         *[jnp.asarray(table) for table in tables],
     )

time: 54.4 us -> 46.6 us (0.86)
  Pallas kernels: 50.1 us -> 43.7 us
  local copies, waits for them, and re-layouts: 3.34 us -> 2 us
    pallas_call x1, Pallas kernels: 50.1 us -> 43.7 us  [local(): pl.pallas_call(functools.partial(kernel, n_gx, n_gy), out_shape=(out, out...]
    reshape x1 -> x0, local copies, waits for them, and re-layouts: 0.69 us -> none  [local(): depth.reshape(slots, 1)]
    unnamed x6 -> x4, local copies, waits for them, and re-layouts: 2.65 us -> 2 us
where the time goes in v1:
time: 46.6 us; the launch traced here: 46.4 us
  Pallas kernels  43.7 us (94%)
  local copies, waits for them, and re-layouts  2 us (4%)
  between operations  0.65 us (1%)
    pallas_call x1, Pallas kernels, local(): pl.pallas_call(functools.partial(kernel, n_gx, n_gy), out_shape=(out, out...  43.7 us
    unnamed x4, local copies, waits for them, and re-layouts  2 us

profile of v1, /device:TPU:1, one launch (start us, length us, event | category | flops | bytes accessed | tf_op | source)
XLA Modules:
  0.0 46.4 jit_solution(722571363042370203)
XLA Ops:
  0.6 43.7 %posterior.1 = (f32[16,512]{1,0:T(8,128)}, f32[16,512]{1,0:T(8,128)}) custom-call(f32[16,512]{1,0:T(8,128)} %bitcast.7, f32[9]{0:T(128)} %stencil_hbm.1, f32[4]{0:T(128)} %mean_hbm.1, f32[4]{0:T(128)} %one_hbm.1, f32[4]{0:T(128)} %two_hbm.1, s32[4]{0:T(128)} %bitcast.10, s32[32]{0:T(128)} %bitcast.11, s32[32,16,128]{2,1,0:T(8,128)} %bitcast.6, ...), custom_call_target="tpu_custom_call" | custom-call | tf_op jit(solution)/shard_map/posterior/pallas_call | solution.py:481
  44.4 0.0 copy-start
  44.4 1.4 %copy.17 = f32[1,16,512]{2,1,0:T(8,128)} copy(f32[1,16,512]{2,1,0:T(8,128)} %bitcast.9) | data formatting | bytes 65536
  45.8 0.0 copy-done
  45.8 0.6 %copy.18 = f32[1,16,512]{2,1,0:T(8,128)} copy(f32[1,16,512]{2,1,0:T(8,128)S(1)} %bitcast.8) | data formatting | bytes 65536
Async XLA Ops:
  44.4 1.4 %copy-start = (f32[16,512]{1,0:T(8,128)S(1)}, f32[16,512]{1,0:T(8,128)}, u32[]{:S(2)}) copy-start(f32[16,512]{1,0:T(8,128)} %get-tuple-element.5) | copy-start | bytes 98308

commit v2 on v1

--- a/solution.py
+++ b/solution.py
@@ -255,7 +255,7 @@
 
 def kernel(
     n_gx, n_gy, noise_hbm, stencil_hbm, mean_hbm, one_hbm, two_hbm, owner_hbm, depth_hbm, counts_ref,
-    w_hbm, cs_hbm, ct_hbm, d8_hbm, tw_hbm, grad_ref, dens_ref,
+    w_hbm, cs_hbm, ct_hbm, d8_hbm, tw_hbm, out_ref,
     noise_ref, stencil_ref, mean_ref, one_ref, two_ref, owner_ref, depth_ref,
     w_ref, cs_ref, ct_ref, d8_ref, tw_ref, in_sem,
     s1, r1, s2, r2, s3, r3, s4, r4, nat, field, frame, dsend, dgot, cgot,
@@ -380,7 +380,7 @@
     main, edge = field_rows(field)
     dens = density_of(main)
     dens_edge = density_of(edge)
-    dens_ref[...] = dens
+    out_ref[1] = dens
     frame[8:24, :] = dens
     frame[7:8, :] = dens_edge[0:1]
     frame[24:25, :] = dens_edge[1:2]
@@ -465,7 +465,7 @@
         for eb in range(4):
             block = r4[pl.ds(64 * eb + xh, 8, stride=8), :]
             nat[72 * eb + 8 * xh : 72 * eb + 8 * xh + 8, :] = turn_vreg(block, roll)
-    grad_ref[...] = rows_inverse(panels(nat, 0, 16), w) - noise_ref[...]
+    out_ref[0] = rows_inverse(panels(nat, 0, 16), w) - noise_ref[...]
 
     for phase, (buf, count) in enumerate(((s1, 2), (s2, 9), (s3, 9), (s4, 2))):
         everything(phase, buf, count).wait_send()
@@ -477,12 +477,11 @@
     rows = noise.shape[1]
     slots = counts.shape[1]
     vmem = pl.BlockSpec(memory_space=pltpu.VMEM)
-    out = jax.ShapeDtypeStruct((rows, NG), F32)
-    grad, dens = pl.pallas_call(
+    both = pl.pallas_call(
         functools.partial(kernel, n_gx, n_gy),
-        out_shape=(out, out),
+        out_shape=jax.ShapeDtypeStruct((2, rows, NG), F32),
         in_specs=[pl.BlockSpec(memory_space=pltpu.HBM)] * 13,
-        out_specs=(vmem, vmem),
+        out_specs=pl.BlockSpec(memory_space=pltpu.VMEM),
         scratch_shapes=[
             pltpu.VMEM((rows, NG), F32),
             pltpu.SMEM((9,), F32),
@@ -512,20 +511,25 @@
             pltpu.SemaphoreType.DMA((3,)),
             pltpu.SemaphoreType.DMA((2,)),
         ],
-        compiler_params=pltpu.CompilerParams(collective_id=0, has_side_effects=True),
+        compiler_params=pltpu.CompilerParams(collective_id=0, has_side_effects=True, vmem_limit_bytes=16 * 1024 * 1024),
         name="posterior",
     )(
-        noise.reshape(rows, NG),
-        stencil,
-        mean_counts,
-        bias_one,
-        bias_two,
-        owner.reshape(-1),
-        depth.reshape(slots),
-        counts.reshape(slots, rows, TC),
-        *[jnp.asarray(table) for table in tables],
+        *[
+            pltpu.with_memory_space_constraint(x, pltpu.HBM)
+            for x in (
+                noise.reshape(rows, NG),
+                stencil,
+                mean_counts,
+                bias_one,
+                bias_two,
+                owner.reshape(-1),
+                depth.reshape(slots),
+                counts.reshape(slots, rows, TC),
+                *[jnp.asarray(table) for table in tables],
+            )
+        ],
     )
-    return grad[None], dens[None]
+    return both[0:1], both[1:2]
 
 
 def solution(mesh):

time: 46.6 us -> 44.5 us (0.955)
  local copies, waits for them, and re-layouts: 2 us -> 0.63 us
  Pallas kernels: 43.7 us -> 43.1 us
    unnamed x4 -> x0, local copies, waits for them, and re-layouts: 2 us -> none
    slice x0 -> x1, local copies, waits for them, and re-layouts: none -> 0.63 us  [local(): return (both[0:1], both[1:2])]
    pallas_call x1, Pallas kernels: 43.7 us -> 43.1 us  [local(): pl.pallas_call(functools.partial(kernel, n_gx, n_gy), out_shape=jax.Shape...]
where the time goes in v2:
time: 44.5 us; the launch traced here: 44.4 us
  Pallas kernels  43.1 us (97%)
  between operations  0.64 us (1%)
  local copies, waits for them, and re-layouts  0.63 us (1%)
    pallas_call x1, Pallas kernels, local(): pl.pallas_call(functools.partial(kernel, n_gx, n_gy), out_shape=jax.Shape...  43.1 us

profile of v2, /device:TPU:1, one launch (start us, length us, event | category | flops | bytes accessed | tf_op | source)
XLA Modules:
  0.0 44.4 jit_solution(8693900841276710098)
XLA Ops:
  0.6 43.1 %posterior.1 = f32[2,16,512]{2,1,0:T(8,128)S(1)} custom-call(f32[16,512]{1,0:T(8,128)} %bitcast.5, f32[9]{0:T(128)} %stencil_hbm.1, f32[4]{0:T(128)} %mean_hbm.1, f32[4]{0:T(128)} %one_hbm.1, f32[4]{0:T(128)} %two_hbm.1, s32[4]{0:T(128)} %bitcast.6, s32[32]{0:T(128)} %bitcast.7, s32[32,16,128]{2,1,0:T(8,128)} %bitcast.4, ...), custom_call_target="tpu_custom_call" | custom-call | tf_op jit(solution)/shard_map/posterior/pallas_call | solution.py:480
  43.8 0.6 %fusion = (f32[1,16,512]{2,1,0:T(8,128)}, f32[1,16,512]{2,1,0:T(8,128)}) fusion(f32[2,16,512]{2,1,0:T(8,128)S(1)} %posterior.1), kind=kLoop, calls=%fused_computation | loop fusion | bytes 131072 | tf_op jit(solution)/shard_map/slice | solution.py:532

commit v3 on v2

--- a/solution.py
+++ b/solution.py
@@ -321,11 +321,11 @@
             block = spec[8 * xh : 8 * xh + 8, 128 * eb : 128 * eb + 128]
             s1[pl.ds(64 * eb + xh, 8, stride=8), :] = turn_vreg(block, roll)
     loads[2].wait()
-    for slot in range(2 * n_gx):
-        dsend[slot // 2, slot % 2 : slot % 2 + 1, :] = jnp.full((1, 128), depth_ref[slot], jnp.int32)
+    left = lax.broadcasted_iota(jnp.int32, (1, 128), 1) < 64
+    for other in range(n_gx):
+        dsend[other, 0:1, :] = jnp.where(left, depth_ref[2 * other], depth_ref[2 * other + 1])
 
     pl.semaphore_wait(barrier, n_gy - 1 + n_gx - 1)
-    exchange(0, s1, r1, 8, 2)
 
     @pl.loop(0, n_gx - 1)
     def _(i):
@@ -338,9 +338,15 @@
             device_id=(to, gy),
             device_id_type=MESH,
         ).start()
+
+    exchange(0, s1, r1, 8, 2)
+
+    @pl.loop(0, n_gx - 1)
+    def _(i):
+        to = lax.rem(gx + far(i), n_gx)
         pltpu.make_async_remote_copy(
-            src_ref=dsend.at[to, pl.ds(0, 2)],
-            dst_ref=dgot.at[gx, pl.ds(0, 2)],
+            src_ref=dsend.at[to, pl.ds(0, 1)],
+            dst_ref=dgot.at[gx, pl.ds(0, 1)],
             send_sem=zsend_sem.at[1],
             recv_sem=zrecv_sem.at[1],
             device_id=(to, gy),
@@ -349,7 +355,7 @@
 
     own = pltpu.make_async_copy(counts_ref.at[pl.ds(2 * gx, 2)], cgot.at[pl.ds(2 * gx, 2)], zsend_sem.at[2])
     own.start()
-    dgot[gx, 0:2, :] = dsend[gx, 0:2, :]
+    dgot[gx, 0:1, :] = dsend[gx, 0:1, :]
 
     flt = filters(gy)
     for load in loads[3:]:
@@ -398,8 +404,8 @@
         device_id_type=MESH,
     )
     got_depth = pltpu.make_async_remote_copy(
-        src_ref=dgot.at[pl.ds(0, n_gx - 1), pl.ds(0, 2)],
-        dst_ref=dgot.at[pl.ds(0, n_gx - 1), pl.ds(0, 2)],
+        src_ref=dgot.at[pl.ds(0, n_gx - 1), pl.ds(0, 1)],
+        dst_ref=dgot.at[pl.ds(0, n_gx - 1), pl.ds(0, 1)],
         send_sem=zsend_sem.at[1],
         recv_sem=zrecv_sem.at[1],
         device_id=(lax.rem(gx + 1, n_gx), gy),
@@ -417,7 +423,9 @@
             rank = rank + jnp.where(owner_ref[t2] == holder, 1, 0)
         seen = cgot[2 * holder + rank].astype(F32)
         classes = dgot[holder]
-        e = jnp.where(rank == 0, classes[0:1, :], classes[1:2, :])
+        row, turned_row = classes[0:1, :], roll(classes, 64, 1)[0:1, :]
+        first, second = jnp.where(left, row, turned_row), jnp.where(left, turned_row, row)
+        e = jnp.where(rank == 0, first, second)
 
         def pick(ref):
             out = jnp.full((1, 128), ref[0], F32)

time: 44.5 us -> 47.1 us (1.058)
  Pallas kernels: 43.1 us -> 45.7 us
    pallas_call x1, Pallas kernels: 43.1 us -> 45.7 us  [local(): pl.pallas_call(functools.partial(kernel, n_gx, n_gy), out_shape=jax.Shape...]
where the time goes in v3:
time: 47.1 us; the launch traced here: 46.9 us
  Pallas kernels  45.7 us (97%)
  between operations  0.64 us (1%)
  local copies, waits for them, and re-layouts  0.63 us (1%)
    pallas_call x1, Pallas kernels, local(): pl.pallas_call(functools.partial(kernel, n_gx, n_gy), out_shape=jax.Shape...  45.7 us

profile of v3, /device:TPU:1, one launch (start us, length us, event | category | flops | bytes accessed | tf_op | source)
XLA Modules:
  0.0 46.9 jit_solution(8494080132981690484)
XLA Ops:
  0.6 45.7 %posterior.1 = f32[2,16,512]{2,1,0:T(8,128)S(1)} custom-call(f32[16,512]{1,0:T(8,128)} %bitcast.5, f32[9]{0:T(128)} %stencil_hbm.1, f32[4]{0:T(128)} %mean_hbm.1, f32[4]{0:T(128)} %one_hbm.1, f32[4]{0:T(128)} %two_hbm.1, s32[4]{0:T(128)} %bitcast.6, s32[32]{0:T(128)} %bitcast.7, s32[32,16,128]{2,1,0:T(8,128)} %bitcast.4, ...), custom_call_target="tpu_custom_call" | custom-call | tf_op jit(solution)/shard_map/posterior/pallas_call | solution.py:488
  46.3 0.6 %fusion = (f32[1,16,512]{2,1,0:T(8,128)}, f32[1,16,512]{2,1,0:T(8,128)}) fusion(f32[2,16,512]{2,1,0:T(8,128)S(1)} %posterior.1), kind=kLoop, calls=%fused_computation | loop fusion | bytes 131072 | tf_op jit(solution)/shard_map/slice | solution.py:540

commit v4 on v3

--- a/solution.py
+++ b/solution.py
@@ -327,19 +327,22 @@
 
     pl.semaphore_wait(barrier, n_gy - 1 + n_gx - 1)
 
-    @pl.loop(0, n_gx - 1)
-    def _(i):
-        to = lax.rem(gx + far(i), n_gx)
-        pltpu.make_async_remote_copy(
-            src_ref=counts_ref.at[pl.ds(2 * to, 2)],
-            dst_ref=cgot.at[pl.ds(2 * gx, 2)],
-            send_sem=zsend_sem.at[0],
-            recv_sem=zrecv_sem.at[0],
-            device_id=(to, gy),
-            device_id_type=MESH,
-        ).start()
-
     exchange(0, s1, r1, 8, 2)
+
+    def send_counts(start, stop):
+        @pl.loop(start, stop)
+        def _(i):
+            to = lax.rem(gx + far(i), n_gx)
+            pltpu.make_async_remote_copy(
+                src_ref=counts_ref.at[pl.ds(2 * to, 2)],
+                dst_ref=cgot.at[pl.ds(2 * gx, 2)],
+                send_sem=zsend_sem.at[0],
+                recv_sem=zrecv_sem.at[0],
+                device_id=(to, gy),
+                device_id_type=MESH,
+            ).start()
+
+    send_counts(0, 8)
 
     @pl.loop(0, n_gx - 1)
     def _(i):
@@ -375,6 +378,7 @@
             s2[pl.ds(2 * f + xh, 32, stride=16), :] = backs[f][32 * xh : 32 * xh + 32]
     s2[pl.ds(8, 32, stride=16), :] = halo_out(backs, roll)
     exchange(1, s2, r2, 16, 9)
+    send_counts(8, n_gx - 1)
 
     everything(1, r2, 9).wait_recv()
     for eb in range(4):

time: 47.1 us -> 45.8 us (0.972)
  Pallas kernels: 45.7 us -> 44.4 us
    pallas_call x1, Pallas kernels: 45.7 us -> 44.4 us  [local(): pl.pallas_call(functools.partial(kernel, n_gx, n_gy), out_shape=jax.Shape...]
where the time goes in v4:
time: 45.8 us; the launch traced here: 45.7 us
  Pallas kernels  44.4 us (97%)
  between operations  0.64 us (1%)
  local copies, waits for them, and re-layouts  0.63 us (1%)
    pallas_call x1, Pallas kernels, local(): pl.pallas_call(functools.partial(kernel, n_gx, n_gy), out_shape=jax.Shape...  44.4 us

profile of v4, /device:TPU:1, one launch (start us, length us, event | category | flops | bytes accessed | tf_op | source)
XLA Modules:
  0.0 45.7 jit_solution(10841946382603830652)
XLA Ops:
  0.6 44.4 %posterior.1 = f32[2,16,512]{2,1,0:T(8,128)S(1)} custom-call(f32[16,512]{1,0:T(8,128)} %bitcast.5, f32[9]{0:T(128)} %stencil_hbm.1, f32[4]{0:T(128)} %mean_hbm.1, f32[4]{0:T(128)} %one_hbm.1, f32[4]{0:T(128)} %two_hbm.1, s32[4]{0:T(128)} %bitcast.6, s32[32]{0:T(128)} %bitcast.7, s32[32,16,128]{2,1,0:T(8,128)} %bitcast.4, ...), custom_call_target="tpu_custom_call" | custom-call | tf_op jit(solution)/shard_map/posterior/pallas_call | solution.py:492
  45.0 0.6 %fusion = (f32[1,16,512]{2,1,0:T(8,128)}, f32[1,16,512]{2,1,0:T(8,128)}) fusion(f32[2,16,512]{2,1,0:T(8,128)S(1)} %posterior.1), kind=kLoop, calls=%fused_computation | loop fusion | bytes 131072 | tf_op jit(solution)/shard_map/slice | solution.py:544
